TPU v7x, 32 devices: a whole 2x2x4 slice. The times are simulated.
32 devices in a mesh: dp: 8 (over z, x), tensor: 4 (over y, core).
Axes of the slice: x: 2, y: 2, z: 4, core: 2. Of those that a mesh axis runs over, the one named last changes fastest.
Arguments:
- inputs: bfloat16 [2, 8, 1024, 1152], P(None, 'dp', 'tensor'), may hold values from -6 to 6
- lengths: int32 [2, 8], P(None, 'dp'), may hold values from 256 to 1024, as said below
- gain_attn: bfloat16 [1152], P('dp'), may hold values from 0.5 to 1.5
- gain_mlp: bfloat16 [1152], P('dp'), may hold values from 0.5 to 1.5
- w_query: bfloat16 [1152, 1152], P('dp'), may hold values from -0.1875 to 0.1875
- key_weight: bfloat16 [1152, 384], P('dp'), may hold values from -0.1875 to 0.1875
- value_weight: bfloat16 [1152, 384], P('dp'), may hold values from -0.1875 to 0.1875
- w_gate: bfloat16 [1152, 3072], P('dp', 'tensor'), may hold values from -0.1875 to 0.1875
- w_up: bfloat16 [1152, 3072], P('dp', 'tensor'), may hold values from -0.1875 to 0.1875
- w_out: bfloat16 [1152, 1152], P('dp'), may hold values from -0.75 to 0.75
- w_down: bfloat16 [3072, 1152], P('tensor', 'dp'), may hold values from -0.21875 to 0.21875
- cotangent: bfloat16 [2, 8, 1024, 1152], P(None, 'dp', 'tensor'), may hold values from -6 to 6
Outputs:
- out_act: bfloat16 [2, 8, 1024, 1152], P(None, 'dp', 'tensor')
- grad_inputs: bfloat16 [2, 8, 1024, 1152], P(None, 'dp', 'tensor')
- grad_gain_attn: float32 [1152], P('dp')
- grad_gain_mlp: float32 [1152], P('dp')
- grad_w_query: float32 [1152, 1152], P('dp')
- grad_w_key: float32 [1152, 384], P('dp')
- grad_w_value: float32 [1152, 384], P('dp')
- grad_w_gate: float32 [1152, 3072], P('dp', 'tensor')
- grad_w_up: float32 [1152, 3072], P('dp', 'tensor')
- grad_w_out: float32 [1152, 1152], P('dp')
- grad_w_down: float32 [3072, 1152], P('tensor', 'dp')
Inputs may be any that keep to these rules, and one draw needn't show every extreme that they name: `lengths`: each sequence's valid tokens; in every micro-batch one sequence fills all 1024 slots.
All inputs are finite; a program needn't handle non-finite values.
Results may differ from a plain program's by a relative error of at most 0.023.
Values may be sent and summed in bfloat16 or wider, within the bound.
No kernel may reach another device: no remote copies, remote signals or barrier semaphores. Data moves between devices by JAX's collectives and lax.ppermute only.
A program may use at most 192 MiB of HBM per device.

v0:
```python
import jax
import jax.numpy as jnp
from jax import lax
from jax.sharding import PartitionSpec as P

HEAD_SIZE = 64
EPSILON = 1e-05
ROPE_BASE = 10000.0
MASKED = -1e30


def rope_tables(positions, head_dim):
    half_dim = head_dim // 2
    exponent = jnp.arange(half_dim, dtype=jnp.float32) * (2.0 / head_dim)
    frequency = ROPE_BASE ** (-exponent)
    angles = positions[:, None] * frequency[None, :]
    cosine_table = jnp.concatenate([jnp.cos(angles), jnp.cos(angles)], axis=1)
    sine_table = jnp.concatenate([jnp.sin(angles), jnp.sin(angles)], axis=1)
    return (cosine_table, sine_table)


def rotate_half(values):
    half_dim = values.shape[-1] // 2
    return jnp.concatenate([-values[..., half_dim:], values[..., :half_dim]], axis=-1)


def apply_rotary(values, cosine_table, sine_table):
    return values * cosine_table[:, None, :] + rotate_half(values) * sine_table[:, None, :]


def unrope(grads_in, cosine_table, sine_table):
    half_dim = grads_in.shape[-1] // 2
    scaled = grads_in * sine_table[:, None, :]
    turned = jnp.concatenate([scaled[..., half_dim:], -scaled[..., :half_dim]], axis=-1)
    return grads_in * cosine_table[:, None, :] + turned


def contract_rows(left_side, right_side):
    return lax.dot_general(
        left_side, right_side, (((0,), (0,)), ((), ())), preferred_element_type=jnp.float32
    )


def contract_last(left_side, right_side):
    return lax.dot_general(
        left_side, right_side, (((1,), (1,)), ((), ())), preferred_element_type=jnp.float32
    )


def fetch_weights(
    gain_attn, gain_mlp, w_query, key_weight, value_weight, w_gate, w_up, w_out, w_down
):
    return (
        lax.all_gather(gain_attn, "dp", axis=0, tiled=True),
        lax.all_gather(gain_mlp, "dp", axis=0, tiled=True),
        lax.all_gather(w_query, "dp", axis=0, tiled=True),
        lax.all_gather(key_weight, "dp", axis=0, tiled=True),
        lax.all_gather(value_weight, "dp", axis=0, tiled=True),
        lax.all_gather(w_gate, "dp", axis=0, tiled=True),
        lax.all_gather(w_up, "dp", axis=0, tiled=True),
        lax.all_gather(w_out, "dp", axis=0, tiled=True),
        lax.all_gather(w_down, "dp", axis=1, tiled=True),
    )


def project_sum(left_side, right_side):
    return lax.psum_scatter(
        jnp.dot(left_side, right_side, preferred_element_type=jnp.float32).astype(jnp.bfloat16),
        "tensor",
        scatter_dimension=0,
        tiled=True,
    ).astype(jnp.float32)


def back_project_sum(pair_list):
    row_share = pair_list[0][0].shape[0] // lax.axis_size("tensor")
    out_width = pair_list[0][1].shape[0]
    summed = jnp.zeros((lax.axis_size("tensor") * row_share, out_width), jnp.float32)
    for grad_part, weight_part in pair_list:
        summed = summed + contract_last(grad_part, weight_part)
    return lax.psum_scatter(
        summed.astype(jnp.bfloat16), "tensor", scatter_dimension=0, tiled=True
    ).astype(jnp.float32)


def reduce_over_data(grad_list):
    (
        grad_query_w,
        grad_key_w,
        grad_value_w,
        grad_gate_w,
        grad_up_w,
        grad_out_w,
        grad_down_w,
        grad_gain_one,
        grad_gain_two,
    ) = grad_list
    return (
        lax.psum_scatter(grad_query_w, "dp", scatter_dimension=0, tiled=True),
        lax.psum_scatter(grad_key_w, "dp", scatter_dimension=0, tiled=True),
        lax.psum_scatter(grad_value_w, "dp", scatter_dimension=0, tiled=True),
        lax.psum_scatter(grad_gate_w, "dp", scatter_dimension=0, tiled=True),
        lax.psum_scatter(grad_up_w, "dp", scatter_dimension=0, tiled=True),
        lax.psum_scatter(grad_out_w, "dp", scatter_dimension=0, tiled=True),
        lax.psum_scatter(grad_down_w, "dp", scatter_dimension=1, tiled=True),
        lax.psum_scatter(grad_gain_one, "dp", scatter_dimension=0, tiled=True),
        lax.psum_scatter(grad_gain_two, "dp", scatter_dimension=0, tiled=True),
    )


def row_scale_of(values):
    return lax.rsqrt(jnp.mean(values * values, axis=-1, keepdims=True) + EPSILON)


def make_mask(query_pos, position_count, valid_count):
    key_pos = jnp.arange(position_count, dtype=jnp.int32)
    return (key_pos[None, :] <= query_pos[:, None]) & (key_pos[None, :] < valid_count)


def attention_scores(query_rows, keys_all, allowed):
    raw_scores = jnp.einsum(
        "qhgd,shd->hgqs", query_rows, keys_all, preferred_element_type=jnp.float32
    ) * HEAD_SIZE ** (-0.5)
    return jnp.where(allowed, raw_scores, MASKED)


def norm_backward(grad_normed, row_values, row_scale, gain_full):
    gain_grad = jnp.sum(grad_normed * row_values * row_scale, axis=0)
    inner_grad = grad_normed * gain_full
    row_grad = row_scale * inner_grad - row_values * row_scale**3 * jnp.mean(
        inner_grad * row_values, axis=-1, keepdims=True
    )
    return (row_grad, gain_grad)


def forward_pass(rows_in, valid_count, weights, row_start):
    (
        gain_attn,
        gain_mlp,
        full_query,
        full_key,
        full_value,
        full_gate,
        full_up,
        full_out,
        full_down,
    ) = weights
    gain_one = gain_attn.astype(jnp.float32)
    gain_two = gain_mlp.astype(jnp.float32)
    row_count = rows_in.shape[0]
    row_values = rows_in.astype(jnp.float32)
    scale_one = row_scale_of(row_values)
    hidden_one = (row_values * scale_one * gain_one).astype(jnp.bfloat16)
    query_heads = full_query.shape[1] // HEAD_SIZE
    key_heads = full_key.shape[1] // HEAD_SIZE
    group_width = query_heads // key_heads
    query_pos = row_start + jnp.arange(row_count, dtype=jnp.int32)
    cosine_table, sine_table = rope_tables(query_pos.astype(jnp.float32), HEAD_SIZE)
    query_unrotated = jnp.dot(hidden_one, full_query, preferred_element_type=jnp.float32).reshape(
        row_count, query_heads, HEAD_SIZE
    )
    key_unrotated = jnp.dot(hidden_one, full_key, preferred_element_type=jnp.float32).reshape(
        row_count, key_heads, HEAD_SIZE
    )
    values_own = jnp.dot(hidden_one, full_value, preferred_element_type=jnp.float32).astype(
        jnp.bfloat16
    )
    query_rows = (
        apply_rotary(query_unrotated, cosine_table, sine_table)
        .astype(jnp.bfloat16)
        .reshape(row_count, key_heads, group_width, HEAD_SIZE)
    )
    keys_own = (
        apply_rotary(key_unrotated, cosine_table, sine_table)
        .astype(jnp.bfloat16)
        .reshape(row_count, key_heads * HEAD_SIZE)
    )
    keys_flat, values_flat = (
        lax.all_gather(keys_own, "tensor", axis=0, tiled=True),
        lax.all_gather(values_own, "tensor", axis=0, tiled=True),
    )
    position_count = keys_flat.shape[0]
    keys_all = keys_flat.reshape(position_count, key_heads, HEAD_SIZE)
    values_all = values_flat.reshape(position_count, key_heads, HEAD_SIZE)
    allowed = make_mask(query_pos, position_count, valid_count)
    scores = attention_scores(query_rows, keys_all, allowed)
    maxima = jnp.max(scores, axis=-1, keepdims=True)
    log_total = maxima + jnp.log(jnp.sum(jnp.exp(scores - maxima), axis=-1, keepdims=True))
    soft_low = jnp.exp(scores - log_total).astype(jnp.bfloat16)
    attended = jnp.einsum(
        "hgqs,shd->qhgd", soft_low, values_all, preferred_element_type=jnp.float32
    )
    attended = attended.reshape(row_count, query_heads * HEAD_SIZE).astype(jnp.bfloat16)
    middle = row_values + jnp.dot(attended, full_out, preferred_element_type=jnp.float32)
    scale_two = row_scale_of(middle)
    hidden_two = lax.all_gather(
        (middle * scale_two * gain_two).astype(jnp.bfloat16), "tensor", axis=0, tiled=True
    )
    gate_proj = jnp.dot(hidden_two, full_gate, preferred_element_type=jnp.float32)
    up_proj = jnp.dot(hidden_two, full_up, preferred_element_type=jnp.float32)
    activated = (jax.nn.silu(gate_proj) * up_proj).astype(jnp.bfloat16)
    ffn_out = project_sum(activated, full_down)
    valid = (query_pos < valid_count).astype(jnp.float32)[:, None]
    output = (valid * (middle + ffn_out)).astype(jnp.bfloat16)
    kept = (
        row_values,
        scale_one,
        hidden_one,
        query_rows,
        keys_all,
        values_all,
        allowed,
        log_total,
        attended,
        middle,
        scale_two,
        hidden_two,
        gate_proj,
        up_proj,
        activated,
        valid,
        cosine_table,
        sine_table,
    )
    return (output, kept)


def backward_pass(cot_rows, weights, kept):
    (
        gain_attn,
        gain_mlp,
        full_query,
        full_key,
        full_value,
        full_gate,
        full_up,
        full_out,
        full_down,
    ) = weights
    (
        row_values,
        scale_one,
        hidden_one,
        query_rows,
        keys_all,
        values_all,
        allowed,
        log_total,
        attended,
        middle,
        scale_two,
        hidden_two,
        gate_proj,
        up_proj,
        activated,
        valid,
        cosine_table,
        sine_table,
    ) = kept
    gain_one = gain_attn.astype(jnp.float32)
    gain_two = gain_mlp.astype(jnp.float32)
    row_count = row_values.shape[0]
    position_count = keys_all.shape[0]
    query_heads = full_query.shape[1] // HEAD_SIZE
    key_heads = full_key.shape[1] // HEAD_SIZE
    group_width = query_heads // key_heads
    grad_rows = cot_rows.astype(jnp.float32) * valid
    grad_ffn = lax.all_gather(grad_rows.astype(jnp.bfloat16), "tensor", axis=0, tiled=True)
    grad_down_w = contract_rows(activated, grad_ffn)
    grad_act = contract_last(grad_ffn, full_down)
    sigmoid_gate = jax.nn.sigmoid(gate_proj)
    grad_gate = (
        grad_act * up_proj * sigmoid_gate * (1.0 + gate_proj * (1.0 - sigmoid_gate))
    ).astype(jnp.bfloat16)
    grad_up = (grad_act * gate_proj * sigmoid_gate).astype(jnp.bfloat16)
    grad_gate_w = contract_rows(hidden_two, grad_gate)
    grad_up_w = contract_rows(hidden_two, grad_up)
    grad_normed_two = back_project_sum(((grad_gate, full_gate), (grad_up, full_up)))
    row_grad_two, grad_gain_two = norm_backward(grad_normed_two, middle, scale_two, gain_two)
    grad_middle = grad_rows + row_grad_two
    grad_branch = grad_middle.astype(jnp.bfloat16)
    grad_out_w = contract_rows(attended, grad_branch)
    grad_att = (
        contract_last(grad_branch, full_out)
        .astype(jnp.bfloat16)
        .reshape(row_count, key_heads, group_width, HEAD_SIZE)
    )
    soft_float = jnp.exp(attention_scores(query_rows, keys_all, allowed) - log_total)
    grad_soft = jnp.einsum(
        "qhgd,shd->hgqs", grad_att, values_all, preferred_element_type=jnp.float32
    )
    grad_scores = (
        soft_float * (grad_soft - jnp.sum(soft_float * grad_soft, axis=-1, keepdims=True))
    ).astype(jnp.bfloat16)
    value_part = jnp.einsum(
        "hgqs,qhgd->shd",
        soft_float.astype(jnp.bfloat16),
        grad_att,
        preferred_element_type=jnp.float32,
    )
    score_scale = HEAD_SIZE ** (-0.5)
    key_part = (
        jnp.einsum("hgqs,qhgd->shd", grad_scores, query_rows, preferred_element_type=jnp.float32)
        * score_scale
    )
    grad_queries = (
        jnp.einsum("hgqs,shd->qhgd", grad_scores, keys_all, preferred_element_type=jnp.float32)
        * score_scale
    )
    grad_queries = (
        unrope(grad_queries.reshape(row_count, query_heads, HEAD_SIZE), cosine_table, sine_table)
        .astype(jnp.bfloat16)
        .reshape(row_count, query_heads * HEAD_SIZE)
    )
    key_own, value_own = (
        lax.psum_scatter(
            key_part.reshape(position_count, key_heads * HEAD_SIZE).astype(jnp.bfloat16),
            "tensor",
            scatter_dimension=0,
            tiled=True,
        ).astype(jnp.float32),
        lax.psum_scatter(
            value_part.reshape(position_count, key_heads * HEAD_SIZE).astype(jnp.bfloat16),
            "tensor",
            scatter_dimension=0,
            tiled=True,
        ).astype(jnp.float32),
    )
    grad_keys = (
        unrope(key_own.reshape(row_count, key_heads, HEAD_SIZE), cosine_table, sine_table)
        .astype(jnp.bfloat16)
        .reshape(row_count, key_heads * HEAD_SIZE)
    )
    grad_values = value_own.astype(jnp.bfloat16)
    grad_query_w = contract_rows(hidden_one, grad_queries)
    grad_key_w = contract_rows(hidden_one, grad_keys)
    grad_value_w = contract_rows(hidden_one, grad_values)
    grad_normed_one = (
        contract_last(grad_queries, full_query)
        + contract_last(grad_keys, full_key)
        + contract_last(grad_values, full_value)
    )
    row_grad_one, grad_gain_one = norm_backward(grad_normed_one, row_values, scale_one, gain_one)
    grad_input = (grad_middle + row_grad_one).astype(jnp.bfloat16)
    return (
        grad_input,
        (
            grad_query_w,
            grad_key_w,
            grad_value_w,
            grad_gate_w,
            grad_up_w,
            grad_out_w,
            grad_down_w,
            grad_gain_one,
            grad_gain_two,
        ),
    )


def shards(
    inputs,
    lengths,
    gain_attn,
    gain_mlp,
    w_query,
    key_weight,
    value_weight,
    w_gate,
    w_up,
    w_out,
    w_down,
    cotangent,
):
    micro_count = inputs.shape[0]
    row_share = inputs.shape[2]
    row_start = lax.axis_index("tensor") * row_share
    outputs = []
    input_grads = []
    grad_totals = None
    for batch_index in range(micro_count):
        current = fetch_weights(
            gain_attn, gain_mlp, w_query, key_weight, value_weight, w_gate, w_up, w_out, w_down
        )
        output, kept = forward_pass(
            inputs[batch_index, 0], lengths[batch_index, 0], current, row_start
        )
        grad_input, batch_grads = backward_pass(cotangent[batch_index, 0], current, kept)
        if batch_index == 0:
            grad_totals = batch_grads
        else:
            grad_totals = jax.tree.map(jnp.add, grad_totals, batch_grads)
        outputs.append(output)
        input_grads.append(grad_input)
    grad_totals = reduce_over_data(grad_totals)
    (
        grad_query_w,
        grad_key_w,
        grad_value_w,
        grad_gate_w,
        grad_up_w,
        grad_out_w,
        grad_down_w,
        grad_gain_one,
        grad_gain_two,
    ) = grad_totals
    grad_query_w, grad_key_w, grad_value_w, grad_out_w, grad_gain_one, grad_gain_two = (
        lax.psum(grad_query_w.astype(jnp.bfloat16), "tensor").astype(jnp.float32),
        lax.psum(grad_key_w.astype(jnp.bfloat16), "tensor").astype(jnp.float32),
        lax.psum(grad_value_w.astype(jnp.bfloat16), "tensor").astype(jnp.float32),
        lax.psum(grad_out_w.astype(jnp.bfloat16), "tensor").astype(jnp.float32),
        lax.psum(grad_gain_one.astype(jnp.bfloat16), "tensor").astype(jnp.float32),
        lax.psum(grad_gain_two.astype(jnp.bfloat16), "tensor").astype(jnp.float32),
    )
    out_stack = jnp.stack(outputs)[:, None]
    grad_stack = jnp.stack(input_grads)[:, None]
    return (
        out_stack,
        grad_stack,
        grad_gain_one,
        grad_gain_two,
        grad_query_w,
        grad_key_w,
        grad_value_w,
        grad_gate_w,
        grad_up_w,
        grad_out_w,
        grad_down_w,
    )


def solution(mesh):
    in_specs = (
        P(None, "dp", "tensor", None),
        P(None, "dp"),
        P("dp"),
        P("dp"),
        P("dp", None),
        P("dp", None),
        P("dp", None),
        P("dp", "tensor"),
        P("dp", "tensor"),
        P("dp", None),
        P("tensor", "dp"),
        P(None, "dp", "tensor", None),
    )
    out_specs = (
        P(None, "dp", "tensor", None),
        P(None, "dp", "tensor", None),
        P("dp"),
        P("dp"),
        P("dp", None),
        P("dp", None),
        P("dp", None),
        P("dp", "tensor"),
        P("dp", "tensor"),
        P("dp", None),
        P("tensor", "dp"),
    )
    return jax.shard_map(shards, mesh=mesh, in_specs=in_specs, out_specs=out_specs, check_vma=False)
```

profile of v0, /device:TPU:0, one launch (start us, length us, event | category | flops | bytes accessed | tf_op | source)
XLA Modules:
  0.0 1362.6 jit_solution(11270381272452233820)
XLA Ops:
  14.7 23.7 %all-reduce.5 = (bf16[1152]{0:T(1024)(128)(2,1)S(1)}, bf16[1152]{0:T(1024)(128)(2,1)S(1)}) all-reduce(bf16[1152]{0:T(1024)(128)(2,1)S(1)} %dynamic-update-slice, bf16[1152]{0:T(1024)(128)(2,1)S(1)} %dynamic-update-slice.1), channel_id=1, replica_groups=mesh['dp'=8,'tensor'=4] {'dp'}, use_global_device_ids=true, to_apply=%add | all-reduce | flops 2304 | bytes 9216
  38.8 34.3 %all_gather.61 = bf16[1152,384]{1,0:T(8,128)(2,1)S(1)} all-gather(bf16[144,384]{1,0:T(8,128)(2,1)S(1)} %copy-done.50), channel_id=1, replica_groups=mesh['dp'=8,'tensor'=4] {'dp'}, dimensions={0}, use_global_device_ids=true | all-gather | bytes 995328 | tf_op jit(solution)/shard_map/all_gather | solution.py:58
  84.6 34.1 %all_gather.63 = bf16[1152,384]{1,0:T(8,128)(2,1)S(1)} all-gather(bf16[144,384]{1,0:T(8,128)(2,1)S(1)} %copy-done.51), channel_id=1, replica_groups=mesh['dp'=8,'tensor'=4] {'dp'}, dimensions={0}, use_global_device_ids=true | all-gather | bytes 995328 | tf_op jit(solution)/shard_map/all_gather | solution.py:57
  188.6 25.0 %all-gather.14.cloned.1.call-done = bf16[1024,1152]{1,0:T(8,128)(2,1)} async-done(((bf16[256,1152]{1,0:T(8,128)(2,1)}), bf16[1024,1152]{1,0:T(8,128)(2,1)}) %all-gather.14.cloned.1.call-update) | async-done | bytes 2359312 | tf_op jit(solution)/shard_map/all_gather | solution.py:196
  219.7 41.9 %all-gather.16.cloned.1.call-done = bf16[1152,768]{1,0:T(8,128)(2,1)} async-done(((bf16[144,768]{1,0:T(8,128)(2,1)}), bf16[1152,768]{1,0:T(8,128)(2,1)}) %all-gather.16.cloned.1.call-update) | async-done | bytes 1769488 | tf_op jit(solution)/shard_map/all_gather | solution.py:59
  267.6 41.0 %all-gather.20.cloned.1.call-done = bf16[768,1152]{0,1:T(8,128)(2,1)} async-done(((bf16[768,144]{0,1:T(8,128)(2,1)}), bf16[768,1152]{0,1:T(8,128)(2,1)}) %all-gather.20.cloned.1.call-update) | async-done | bytes 1769488 | tf_op jit(solution)/shard_map/all_gather | solution.py:62
  308.6 25.3 %all-gather.24.cloned.1.call-done = bf16[1024,1152]{1,0:T(8,128)(2,1)} async-done(((bf16[256,1152]{1,0:T(8,128)(2,1)}), bf16[1024,1152]{1,0:T(8,128)(2,1)}) %all-gather.24.cloned.1.call-update) | async-done | bytes 2359312 | tf_op jit(solution)/shard_map/all_gather | solution.py:268
  410.5 23.5 %all-gather.22.cloned.1.call-done = bf16[1024,1152]{1,0:T(8,128)(2,1)} async-done(((bf16[256,1152]{1,0:T(8,128)(2,1)}), bf16[1024,1152]{1,0:T(8,128)(2,1)}) %all-gather.22.cloned.1.call-update) | async-done | bytes 2359312 | tf_op jit(solution)/shard_map/all_gather | solution.py:196
  444.0 15.5 %all-gather.26.cloned.1.call-done = bf16[1024,1152]{1,0:T(8,128)(2,1)} async-done(((bf16[256,1152]{1,0:T(8,128)(2,1)}), bf16[1024,1152]{1,0:T(8,128)(2,1)}) %all-gather.26.cloned.1.call-update) | async-done | bytes 2359312 | tf_op jit(solution)/shard_map/all_gather | solution.py:268
  487.6 19.8 %reduce-scatter.26.cloned.1.call-done = bf16[256,1152]{1,0:T(8,128)(2,1)} async-done(((bf16[1024,1152]{1,0:T(8,128)(2,1)}), bf16[256,1152]{1,0:T(8,128)(2,1)}) %reduce-scatter.26.cloned.1.call-update) | async-done | bytes 589840 | tf_op jit(solution)/shard_map/reduce_scatter | solution.py:81
  510.0 32.9 %reduce-scatter.16.cloned.1.call-done = bf16[256,1152]{1,0:T(8,128)(2,1)} async-done(((bf16[1024,1152]{1,0:T(8,128)(2,1)}), bf16[256,1152]{1,0:T(8,128)(2,1)}) %reduce-scatter.16.cloned.1.call-update) | async-done | bytes 589840 | tf_op jit(solution)/shard_map/reduce_scatter | solution.py:67
  542.9 35.8 %reduce-scatter.18.cloned.1.call-done = bf16[256,1152]{1,0:T(8,128)(2,1)} async-done(((bf16[1024,1152]{1,0:T(8,128)(2,1)}), bf16[256,1152]{1,0:T(8,128)(2,1)}) %reduce-scatter.18.cloned.1.call-update) | async-done | bytes 589840 | tf_op jit(solution)/shard_map/reduce_scatter | solution.py:67
  631.2 13.6 fusion.2
  652.2 12.8 fusion.3
  665.2 13.6 fusion.5
  689.1 25.8 %reduce-scatter.22.cloned.1.call-done = bf16[256,384]{0,1:T(8,128)(2,1)} async-done(((bf16[1024,384]{0,1:T(8,128)(2,1)}), bf16[256,384]{0,1:T(8,128)(2,1)}) %reduce-scatter.22.cloned.1.call-update) | async-done | bytes 196624 | tf_op jit(solution)/shard_map/reduce_scatter | solution.py:316
  751.3 33.2 %reduce-scatter.36.cloned.1.call-done = f32[144,384]{1,0:T(8,128)} async-done(((f32[1152,384]{1,0:T(8,128)}), f32[144,384]{1,0:T(8,128)}) %reduce-scatter.36.cloned.1.call-update) | async-done | bytes 221200 | tf_op jit(solution)/shard_map/reduce_scatter | solution.py:101
  786.1 67.5 %reduce-scatter.34.cloned.1.call-done = f32[144,384]{1,0:T(8,128)} async-done(((f32[1152,384]{1,0:T(8,128)}), f32[144,384]{1,0:T(8,128)}) %reduce-scatter.34.cloned.1.call-update) | async-done | bytes 221200 | tf_op jit(solution)/shard_map/reduce_scatter | solution.py:100
  855.2 104.9 %reduce-scatter.42.cloned.1.call-done = f32[144,1152]{1,0:T(8,128)} async-done(((f32[1152,1152]{1,0:T(8,128)}), f32[144,1152]{1,0:T(8,128)}) %reduce-scatter.42.cloned.1.call-update) | async-done | bytes 663568 | tf_op jit(solution)/shard_map/reduce_scatter | solution.py:104
  962.0 106.2 %reduce-scatter.32.cloned.1.call-done = f32[144,1152]{1,0:T(8,128)} async-done(((f32[1152,1152]{1,0:T(8,128)}), f32[144,1152]{1,0:T(8,128)}) %reduce-scatter.32.cloned.1.call-update) | async-done | bytes 663568 | tf_op jit(solution)/shard_map/reduce_scatter | solution.py:99
  1107.6 37.4 %all-reduce.4 = (bf16[1152]{0:T(1024)(128)(2,1)}, bf16[1152]{0:T(1024)(128)(2,1)}) all-reduce(f32[1152]{0:T(1024)} %add.291, f32[1152]{0:T(1024)} %add.292), channel_id=10, replica_groups=mesh['dp'=8,'tensor'=4] {'dp'}, use_global_device_ids=true, to_apply=%region_24.25.clone | all-reduce | flops 2304 | bytes 13824
  1167.3 23.0 %reduce-scatter.38.cloned.1.call-done = f32[144,768]{1,0:T(8,128)} async-done(((f32[1152,768]{1,0:T(8,128)}), f32[144,768]{1,0:T(8,128)}) %reduce-scatter.38.cloned.1.call-update) | async-done | bytes 442384 | tf_op jit(solution)/shard_map/reduce_scatter | solution.py:102
  1190.3 82.8 %reduce-scatter.40.cloned.1.call-done = f32[144,768]{1,0:T(8,128)} async-done(((f32[1152,768]{1,0:T(8,128)}), f32[144,768]{1,0:T(8,128)}) %reduce-scatter.40.cloned.1.call-update) | async-done | bytes 442384 | tf_op jit(solution)/shard_map/reduce_scatter | solution.py:103
  1273.2 82.7 %reduce-scatter.44.cloned.1.call-done = f32[768,144]{0,1:T(8,128)} async-done(((f32[768,1152]{0,1:T(8,128)}), f32[768,144]{0,1:T(8,128)}) %reduce-scatter.44.cloned.1.call-update) | async-done | bytes 442384 | tf_op jit(solution)/shard_map/reduce_scatter | solution.py:105
  (355 shorter events, 389.8 us)
Async XLA Ops:
  7.2 124.0 %all-gather.10.cloned.1.call-start = ((), (), s32[]{:S(2)}) async-start(), calls=%async_computation.15 | async-start | bytes 2985984 | tf_op jit(solution)/shard_map/all_gather | solution.py:56
  8.0 161.3 %all-gather.12.cloned.1.call-start = ((), (), s32[]{:S(2)}) async-start(), calls=%async_computation.16 | async-start | bytes 2985984 | tf_op jit(solution)/shard_map/all_gather | solution.py:61
  8.7 179.8 %all-gather.18.cloned.1.call-start = ((), (), s32[]{:S(2)}) async-start(), calls=%async_computation.19 | async-start | bytes 1990656 | tf_op jit(solution)/shard_map/all_gather | solution.py:60
  9.5 204.1 %all-gather.14.cloned.1.call-start = ((), (), s32[]{:S(2)}) async-start(), calls=%async_computation.17 | async-start | bytes 2949120 | tf_op jit(solution)/shard_map/all_gather | solution.py:196
  174.0 87.6 %all-gather.16.cloned.1.call-start = ((), (), s32[]{:S(2)}) async-start(), calls=%async_computation.18 | async-start | bytes 1990656 | tf_op jit(solution)/shard_map/all_gather | solution.py:59
  174.6 134.0 %all-gather.20.cloned.1.call-start = ((), (), s32[]{:S(2)}) async-start(), calls=%async_computation.20 | async-start | bytes 1990656 | tf_op jit(solution)/shard_map/all_gather | solution.py:62
  175.1 158.7 %all-gather.24.cloned.1.call-start = ((), (), s32[]{:S(2)}) async-start(), calls=%async_computation.24 | async-start | bytes 2949120 | tf_op jit(solution)/shard_map/all_gather | solution.py:268
  179.3 227.0 %reduce-scatter.20.cloned.1.call-start = ((), (), s32[]{:S(2)}) async-start(), calls=%async_computation.25 | async-start | bytes 2949120 | tf_op jit(solution)/shard_map/reduce_scatter | solution.py:81
  348.5 85.5 %all-gather.22.cloned.1.call-start = ((), (), s32[]{:S(2)}) async-start(), calls=%async_computation.22 | async-start | bytes 2949120 | tf_op jit(solution)/shard_map/all_gather | solution.py:196
  409.7 49.9 %all-gather.26.cloned.1.call-start = ((), (), s32[]{:S(2)}) async-start(), calls=%async_computation.28 | async-start | bytes 2949120 | tf_op jit(solution)/shard_map/all_gather | solution.py:268
  410.2 97.2 %reduce-scatter.26.cloned.1.call-start = ((), (), s32[]{:S(2)}) async-start(), calls=%async_computation.29 | async-start | bytes 2949120 | tf_op jit(solution)/shard_map/reduce_scatter | solution.py:81
  474.2 68.7 %reduce-scatter.16.cloned.1.call-start = ((), (), s32[]{:S(2)}) async-start(), calls=%async_computation.21 | async-start | bytes 2949120 | tf_op jit(solution)/shard_map/reduce_scatter | solution.py:67
  479.9 98.8 %reduce-scatter.18.cloned.1.call-start = ((), (), s32[]{:S(2)}) async-start(), calls=%async_computation.23 | async-start | bytes 2949120 | tf_op jit(solution)/shard_map/reduce_scatter | solution.py:67
  486.3 196.6 %reduce-scatter.24.cloned.1.call-start = ((), (), s32[]{:S(2)}) async-start(), calls=%async_computation.27 | async-start | bytes 983040 | tf_op jit(solution)/shard_map/reduce_scatter | solution.py:322
  605.9 79.7 %reduce-scatter.30.cloned.1.call-start = ((), (), s32[]{:S(2)}) async-start(), calls=%async_computation.31 | async-start | bytes 983040 | tf_op jit(solution)/shard_map/reduce_scatter | solution.py:322
  631.0 58.2 %reduce-scatter.28.cloned.1.call-start = ((), (), s32[]{:S(2)}) async-start(), calls=%async_computation.30 | async-start | bytes 983040 | tf_op jit(solution)/shard_map/reduce_scatter | solution.py:316
  682.8 101.7 %reduce-scatter.36.cloned.1.call-start = ((), (), s32[]{:S(2)}) async-start(), calls=%async_computation.34 | async-start | bytes 1990656 | tf_op jit(solution)/shard_map/reduce_scatter | solution.py:101
  689.1 164.5 %reduce-scatter.34.cloned.1.call-start = ((), (), s32[]{:S(2)}) async-start(), calls=%async_computation.33 | async-start | bytes 1990656 | tf_op jit(solution)/shard_map/reduce_scatter | solution.py:100
  719.6 240.5 %reduce-scatter.42.cloned.1.call-start = ((), (), s32[]{:S(2)}) async-start(), calls=%async_computation.37 | async-start | bytes 5971968 | tf_op jit(solution)/shard_map/reduce_scatter | solution.py:104
  725.4 342.8 %reduce-scatter.32.cloned.1.call-start = ((), (), s32[]{:S(2)}) async-start(), calls=%async_computation.32 | async-start | bytes 5971968 | tf_op jit(solution)/shard_map/reduce_scatter | solution.py:99
  745.3 416.1 %all-reduce.10.cloned.1.call-start = ((), (), s32[]{:S(2)}) async-start(), calls=%async_computation.39 | async-start | bytes 1769472 | tf_op jit(solution)/shard_map/psum | solution.py:408
  1070.0 120.3 %reduce-scatter.38.cloned.1.call-start = ((), (), s32[]{:S(2)}) async-start(), calls=%async_computation.35 | async-start | bytes 3981312 | tf_op jit(solution)/shard_map/reduce_scatter | solution.py:102
  1077.1 196.0 %reduce-scatter.40.cloned.1.call-start = ((), (), s32[]{:S(2)}) async-start(), calls=%async_computation.36 | async-start | bytes 3981312 | tf_op jit(solution)/shard_map/reduce_scatter | solution.py:103
  1085.6 270.2 %reduce-scatter.44.cloned.1.call-start = ((), (), s32[]{:S(2)}) async-start(), calls=%async_computation.38 | async-start | bytes 3981312 | tf_op jit(solution)/shard_map/reduce_scatter | solution.py:105
  (84 other events, 2173.2 us)
Sparse Core Ops, SparseCore 0:
  10.2 70.2 all-gather.9
  82.7 58.9 all-gather.11
  143.9 44.6 all-gather.17
  215.6 45.9 all-gather.15
  263.6 44.9 all-gather.19
  310.7 23.0 all-gather.23
  348.6 35.2 reduce-scatter.19
  409.8 24.1 all-gather.21
  435.4 24.0 all-gather.25
  474.3 33.0 reduce-scatter.25
  509.8 33.0 reduce-scatter.15
  545.6 33.0 reduce-scatter.17
  606.0 23.2 reduce-scatter.23
  631.9 23.2 reduce-scatter.29
  665.2 23.2 reduce-scatter.27
  691.6 23.2 reduce-scatter.21
  718.2 66.2 reduce-scatter.35
  788.4 65.1 reduce-scatter.33
  857.0 103.0 reduce-scatter.41
  964.2 103.9 reduce-scatter.31
  1071.3 35.1 all-reduce.9
  1110.7 79.6 reduce-scatter.37
  1194.4 78.7 reduce-scatter.39
  1277.4 78.4 reduce-scatter.43
  (1 shorter events, 22.9 us)
where the time goes:
time: 1370 us; the launch traced here: 1360 us
  waiting for transfers between devices  800 us (58%)
  matrix products  238 us (17%)
  blocking collectives  173 us (13%)
  other arithmetic  102 us (7%)
  local copies, waits for them, and re-layouts  30.1 us (2%)
  between operations  16.6 us (1%)
    reduce_scatter x1, waiting for transfers between devices, reduce_over_data(): lax.psum_scatter(grad_query_w, 'dp', scatter_dimension=0, tiled=True)  106 us
    reduce_scatter x1, waiting for transfers between devices, reduce_over_data(): lax.psum_scatter(grad_out_w, 'dp', scatter_dimension=0, tiled=True)  105 us
    reduce_scatter x1, waiting for transfers between devices, reduce_over_data(): lax.psum_scatter(grad_up_w, 'dp', scatter_dimension=0, tiled=True)  82.8 us
    reduce_scatter x1, waiting for transfers between devices, reduce_over_data(): lax.psum_scatter(grad_down_w, 'dp', scatter_dimension=1, tiled=True)  82.7 us
    reduce_scatter x2, waiting for transfers between devices, project_sum(): lax.psum_scatter(jnp.dot(left_side, right_side, preferred_element_type=jn...  68.7 us
    reduce_scatter x1, waiting for transfers between devices, reduce_over_data(): lax.psum_scatter(grad_key_w, 'dp', scatter_dimension=0, tiled=True)  67.5 us
    unnamed x2, blocking collectives  61.1 us
    all_gather x2, waiting for transfers between devices, forward_pass(): lax.all_gather((middle * scale_two * gain_two).astype(jnp.bfloat16), 'ten...  48.5 us
  transfers between devices with their start and end apart: 25, of which 18 were waited for; matrix products, arithmetic and copies ran while one was open for 22% of the time, Pallas kernels for 0%

commit v1 on v0

--- a/solution.py
+++ b/solution.py
@@ -7,6 +7,28 @@
 EPSILON = 1e-05
 ROPE_BASE = 10000.0
 MASKED = -1e30
+
+
+def refer_spot(mat, dim_k):
+    net_axis = "dp"
+    work_now = lax.axis_size(net_axis)
+    w1, field_out, upper = (work_now, lax.axis_index(net_axis), mat.shape[dim_k])
+    steps_seen = [w * w1 if j == dim_k else w for j, w in enumerate(mat.shape)]
+    k_now = lax.dynamic_update_slice_in_dim(
+        jnp.zeros(steps_seen, mat.dtype), mat, field_out * upper, axis=dim_k
+    )
+    reached = y = mat
+    for i in [*range(1, w1 // 2 + 1)]:
+        reached = lax.ppermute(reached, net_axis, [(j, (j + 1) % w1) for j in range(w1)])
+        k_now = lax.dynamic_update_slice_in_dim(
+            k_now, reached, (field_out - i) % w1 * upper, axis=dim_k
+        )
+        if 2 * i < w1:
+            y = lax.ppermute(y, net_axis, [(j, (j - 1) % w1) for j in range(w1)])
+            k_now = lax.dynamic_update_slice_in_dim(
+                k_now, y, (field_out + i) % w1 * upper, axis=dim_k
+            )
+    return k_now
 
 
 def rope_tables(positions, head_dim):
@@ -59,7 +81,7 @@
         lax.all_gather(w_gate, "dp", axis=0, tiled=True),
         lax.all_gather(w_up, "dp", axis=0, tiled=True),
         lax.all_gather(w_out, "dp", axis=0, tiled=True),
-        lax.all_gather(w_down, "dp", axis=1, tiled=True),
+        refer_spot(w_down, 1),
     )
 
 

time: 1370 us -> 1330 us (0.971)
  waiting for transfers between devices: 800 us -> 735 us
  starting transfers between devices: 2.57 us -> 17.4 us
    all_gather x1 -> x0, waiting for transfers between devices: 41 us -> none  [fetch_weights(): lax.all_gather(w_down, 'dp', axis=1, tiled=True)]
    all_gather x2, waiting for transfers between devices: 48.5 us -> 23.3 us  [forward_pass(): lax.all_gather((middle * scale_two * gain_two).astype(jnp.bfloat16), 'ten...]
    ppermute x0 -> x7, waiting for transfers between devices: none -> 23.5 us  [the longest x4 15 us: refer_spot(): lax.ppermute(reached, net_axis, [(j, (j + 1) % w1) for j in range(w1)])]
    ppermute x0 -> x7, starting transfers between devices: none -> 14.9 us  [the longest x3 11.8 us: refer_spot(): y = lax.ppermute(y, net_axis, [(j, (j - 1) % w1) for j in range(w1)])]
  transfers between devices with their start and end apart: 25 -> 31, of which waited for: 18 -> 20; matrix products, arithmetic and copies ran while one was open for 22% -> 23% of each run, Pallas kernels for 0% -> 0%
where the time goes in v1:
time: 1330 us; the launch traced here: 1320 us
  waiting for transfers between devices  735 us (55%)
  matrix products  238 us (18%)
  blocking collectives  174 us (13%)
  other arithmetic  102 us (8%)
  local copies, waits for them, and re-layouts  39.1 us (3%)
  starting transfers between devices  17.4 us (1%)
  between operations  17 us (1%)
    reduce_scatter x1, waiting for transfers between devices, reduce_over_data(): lax.psum_scatter(grad_query_w, 'dp', scatter_dimension=0, tiled=True)  106 us
    reduce_scatter x1, waiting for transfers between devices, reduce_over_data(): lax.psum_scatter(grad_out_w, 'dp', scatter_dimension=0, tiled=True)  105 us
    reduce_scatter x1, waiting for transfers between devices, reduce_over_data(): lax.psum_scatter(grad_down_w, 'dp', scatter_dimension=1, tiled=True)  82.7 us
    reduce_scatter x1, waiting for transfers between devices, reduce_over_data(): lax.psum_scatter(grad_up_w, 'dp', scatter_dimension=0, tiled=True)  82.7 us
    reduce_scatter x2, waiting for transfers between devices, project_sum(): lax.psum_scatter(jnp.dot(left_side, right_side, preferred_element_type=jn...  68.7 us
    reduce_scatter x1, waiting for transfers between devices, reduce_over_data(): lax.psum_scatter(grad_key_w, 'dp', scatter_dimension=0, tiled=True)  67.3 us
    unnamed x2, blocking collectives  61 us
    dot_general x14, matrix products, contract_rows(): lax.dot_general(left_side, right_side, (((0,), (0,)), ((), ())), preferre...  46.9 us
  transfers between devices with their start and end apart: 31, of which 20 were waited for; matrix products, arithmetic and copies ran while one was open for 23% of the time, Pallas kernels for 0%

profile of v1, /device:TPU:0, one launch (start us, length us, event | category | flops | bytes accessed | tf_op | source)
XLA Modules:
  0.0 1321.5 jit_solution(9649227401611040573)
XLA Ops:
  14.8 23.7 %all-reduce.5 = (bf16[1152]{0:T(1024)(128)(2,1)S(1)}, bf16[1152]{0:T(1024)(128)(2,1)S(1)}) all-reduce(bf16[1152]{0:T(1024)(128)(2,1)S(1)} %dynamic-update-slice, bf16[1152]{0:T(1024)(128)(2,1)S(1)} %dynamic-update-slice.1), channel_id=1, replica_groups=mesh['dp'=8,'tensor'=4] {'dp'}, use_global_device_ids=true, to_apply=%add | all-reduce | flops 2304 | bytes 9216
  38.8 34.4 %all_gather.57 = bf16[1152,384]{1,0:T(8,128)(2,1)S(1)} all-gather(bf16[144,384]{1,0:T(8,128)(2,1)S(1)} %copy-done.51), channel_id=1, replica_groups=mesh['dp'=8,'tensor'=4] {'dp'}, dimensions={0}, use_global_device_ids=true | all-gather | bytes 995328 | tf_op jit(solution)/shard_map/all_gather | solution.py:80
  84.8 34.3 %all_gather.59 = bf16[1152,384]{1,0:T(8,128)(2,1)S(1)} all-gather(bf16[144,384]{1,0:T(8,128)(2,1)S(1)} %copy-done.52), channel_id=1, replica_groups=mesh['dp'=8,'tensor'=4] {'dp'}, dimensions={0}, use_global_device_ids=true | all-gather | bytes 995328 | tf_op jit(solution)/shard_map/all_gather | solution.py:79
  232.4 35.7 %all-gather.15.cloned.1.call-done = bf16[1152,768]{1,0:T(8,128)(2,1)} async-done(((bf16[144,768]{1,0:T(8,128)(2,1)}), bf16[1152,768]{1,0:T(8,128)(2,1)}) %all-gather.15.cloned.1.call-update) | async-done | bytes 1769488 | tf_op jit(solution)/shard_map/all_gather | solution.py:81
  274.1 19.0 %all-gather.21.cloned.1.call-done = bf16[1024,1152]{1,0:T(8,128)(2,1)} async-done(((bf16[256,1152]{1,0:T(8,128)(2,1)}), bf16[1024,1152]{1,0:T(8,128)(2,1)}) %all-gather.21.cloned.1.call-update) | async-done | bytes 2359312 | tf_op jit(solution)/shard_map/all_gather | solution.py:290
  369.9 23.3 %all-gather.19.cloned.1.call-done = bf16[1024,1152]{1,0:T(8,128)(2,1)} async-done(((bf16[256,1152]{1,0:T(8,128)(2,1)}), bf16[1024,1152]{1,0:T(8,128)(2,1)}) %all-gather.19.cloned.1.call-update) | async-done | bytes 2359312 | tf_op jit(solution)/shard_map/all_gather | solution.py:218
  403.2 15.7 %all-gather.23.cloned.1.call-done = bf16[1024,1152]{1,0:T(8,128)(2,1)} async-done(((bf16[256,1152]{1,0:T(8,128)(2,1)}), bf16[1024,1152]{1,0:T(8,128)(2,1)}) %all-gather.23.cloned.1.call-update) | async-done | bytes 2359312 | tf_op jit(solution)/shard_map/all_gather | solution.py:290
  447.1 19.7 %reduce-scatter.26.cloned.1.call-done = bf16[256,1152]{1,0:T(8,128)(2,1)} async-done(((bf16[1024,1152]{1,0:T(8,128)(2,1)}), bf16[256,1152]{1,0:T(8,128)(2,1)}) %reduce-scatter.26.cloned.1.call-update) | async-done | bytes 589840 | tf_op jit(solution)/shard_map/reduce_scatter | solution.py:103
  469.4 33.1 %reduce-scatter.16.cloned.1.call-done = bf16[256,1152]{1,0:T(8,128)(2,1)} async-done(((bf16[1024,1152]{1,0:T(8,128)(2,1)}), bf16[256,1152]{1,0:T(8,128)(2,1)}) %reduce-scatter.16.cloned.1.call-update) | async-done | bytes 589840 | tf_op jit(solution)/shard_map/reduce_scatter | solution.py:89
  502.4 35.6 %reduce-scatter.18.cloned.1.call-done = bf16[256,1152]{1,0:T(8,128)(2,1)} async-done(((bf16[1024,1152]{1,0:T(8,128)(2,1)}), bf16[256,1152]{1,0:T(8,128)(2,1)}) %reduce-scatter.18.cloned.1.call-update) | async-done | bytes 589840 | tf_op jit(solution)/shard_map/reduce_scatter | solution.py:89
  565.3 12.2 bitcast_convert_fusion
  577.5 12.7 fusion
  590.5 13.6 %fusion.2 = bf16[6,3,256,1024]{2,3,1,0:T(8,128)(2,1)S(1)} fusion(f32[6,1024,256,3]{2,1,3,0:T(8,128)} %get-tuple-element.142, f32[6,1024,256,3]{2,1,3,0:T(8,128)} %get-tuple-element.136, f32[6,3,256]{2,1,0:T(4,128)S(1)} %get-tuple-element.141, f32[6,3,256]{2,1,0:T(4,128)S(1)} %log_add_fusion, pred[256,1024]{0,1:T(8,128)(4,1)S(1)} %get-tuple-element.126), kind=kLoop, calls=%fused_computation.4 | loop fusion | flops 28311552 | bytes 47484928 | tf_op jit(solution)/shard_map/convert_element_type | solution.py:316
  611.5 12.8 fusion.3
  624.4 13.6 %fusion.5 = bf16[6,3,256,1024]{2,3,1,0:T(8,128)(2,1)S(1)} fusion(f32[6,1024,256,3]{2,1,3,0:T(8,128)} %get-tuple-element.140, f32[6,1024,256,3]{2,1,3,0:T(8,128)} %get-tuple-element.132, f32[6,3,256]{2,1,0:T(4,128)S(1)} %get-tuple-element.139, f32[6,3,256]{2,1,0:T(4,128)S(1)} %log_add_fusion.1, pred[256,1024]{0,1:T(8,128)(4,1)S(1)} %get-tuple-element.125), kind=kLoop, calls=%fused_computation.9 | loop fusion | flops 28311552 | bytes 47484928 | tf_op jit(solution)/shard_map/convert_element_type | solution.py:316
  648.3 25.8 %reduce-scatter.22.cloned.1.call-done = bf16[256,384]{0,1:T(8,128)(2,1)} async-done(((bf16[1024,384]{0,1:T(8,128)(2,1)}), bf16[256,384]{0,1:T(8,128)(2,1)}) %reduce-scatter.22.cloned.1.call-update) | async-done | bytes 196624 | tf_op jit(solution)/shard_map/reduce_scatter | solution.py:338
  710.6 32.8 %reduce-scatter.36.cloned.1.call-done = f32[144,384]{1,0:T(8,128)} async-done(((f32[1152,384]{1,0:T(8,128)}), f32[144,384]{1,0:T(8,128)}) %reduce-scatter.36.cloned.1.call-update) | async-done | bytes 221200 | tf_op jit(solution)/shard_map/reduce_scatter | solution.py:123
  745.0 67.3 %reduce-scatter.34.cloned.1.call-done = f32[144,384]{1,0:T(8,128)} async-done(((f32[1152,384]{1,0:T(8,128)}), f32[144,384]{1,0:T(8,128)}) %reduce-scatter.34.cloned.1.call-update) | async-done | bytes 221200 | tf_op jit(solution)/shard_map/reduce_scatter | solution.py:122
  813.8 105.1 %reduce-scatter.42.cloned.1.call-done = f32[144,1152]{1,0:T(8,128)} async-done(((f32[1152,1152]{1,0:T(8,128)}), f32[144,1152]{1,0:T(8,128)}) %reduce-scatter.42.cloned.1.call-update) | async-done | bytes 663568 | tf_op jit(solution)/shard_map/reduce_scatter | solution.py:126
  920.8 106.0 %reduce-scatter.32.cloned.1.call-done = f32[144,1152]{1,0:T(8,128)} async-done(((f32[1152,1152]{1,0:T(8,128)}), f32[144,1152]{1,0:T(8,128)}) %reduce-scatter.32.cloned.1.call-update) | async-done | bytes 663568 | tf_op jit(solution)/shard_map/reduce_scatter | solution.py:121
  1066.3 37.3 %all-reduce.4 = (bf16[1152]{0:T(1024)(128)(2,1)}, bf16[1152]{0:T(1024)(128)(2,1)}) all-reduce(f32[1152]{0:T(1024)} %add.386, f32[1152]{0:T(1024)} %add.387), channel_id=10, replica_groups=mesh['dp'=8,'tensor'=4] {'dp'}, use_global_device_ids=true, to_apply=%region_24.25.clone | all-reduce | flops 2304 | bytes 13824
  1126.0 23.1 %reduce-scatter.38.cloned.1.call-done = f32[144,768]{1,0:T(8,128)} async-done(((f32[1152,768]{1,0:T(8,128)}), f32[144,768]{1,0:T(8,128)}) %reduce-scatter.38.cloned.1.call-update) | async-done | bytes 442384 | tf_op jit(solution)/shard_map/reduce_scatter | solution.py:124
  1149.1 82.7 %reduce-scatter.40.cloned.1.call-done = f32[144,768]{1,0:T(8,128)} async-done(((f32[1152,768]{1,0:T(8,128)}), f32[144,768]{1,0:T(8,128)}) %reduce-scatter.40.cloned.1.call-update) | async-done | bytes 442384 | tf_op jit(solution)/shard_map/reduce_scatter | solution.py:125
  1231.8 82.7 %reduce-scatter.44.cloned.1.call-done = f32[768,144]{0,1:T(8,128)} async-done(((f32[768,1152]{0,1:T(8,128)}), f32[768,144]{0,1:T(8,128)}) %reduce-scatter.44.cloned.1.call-update) | async-done | bytes 442384 | tf_op jit(solution)/shard_map/reduce_scatter | solution.py:127
  (377 shorter events, 402.3 us)
Async XLA Ops:
  7.2 124.3 %all-gather.9.cloned.1.call-start = ((), (), s32[]{:S(2)}) async-start(), calls=%async_computation.15 | async-start | bytes 2985984 | tf_op jit(solution)/shard_map/all_gather | solution.py:78
  8.0 161.5 %all-gather.11.cloned.1.call-start = ((), (), s32[]{:S(2)}) async-start(), calls=%async_computation.16 | async-start | bytes 2985984 | tf_op jit(solution)/shard_map/all_gather | solution.py:83
  8.7 217.5 %all-gather.17.cloned.1.call-start = ((), (), s32[]{:S(2)}) async-start(), calls=%async_computation.19 | async-start | bytes 1990656 | tf_op jit(solution)/shard_map/all_gather | solution.py:82
  9.5 216.8 %all-gather.13.cloned.1.call-start = ((), (), s32[]{:S(2)}) async-start(), calls=%async_computation.17 | async-start | bytes 2949120 | tf_op jit(solution)/shard_map/all_gather | solution.py:218
  174.2 93.8 %all-gather.15.cloned.1.call-start = ((), (), s32[]{:S(2)}) async-start(), calls=%async_computation.18 | async-start | bytes 1990656 | tf_op jit(solution)/shard_map/all_gather | solution.py:81
  174.8 118.4 %all-gather.21.cloned.1.call-start = ((), (), s32[]{:S(2)}) async-start(), calls=%async_computation.23 | async-start | bytes 2949120 | tf_op jit(solution)/shard_map/all_gather | solution.py:290
  178.9 186.6 %reduce-scatter.20.cloned.1.call-start = ((), (), s32[]{:S(2)}) async-start(), calls=%async_computation.24 | async-start | bytes 2949120 | tf_op jit(solution)/shard_map/reduce_scatter | solution.py:103
  307.8 85.4 %all-gather.19.cloned.1.call-start = ((), (), s32[]{:S(2)}) async-start(), calls=%async_computation.21 | async-start | bytes 2949120 | tf_op jit(solution)/shard_map/all_gather | solution.py:218
  368.9 50.0 %all-gather.23.cloned.1.call-start = ((), (), s32[]{:S(2)}) async-start(), calls=%async_computation.27 | async-start | bytes 2949120 | tf_op jit(solution)/shard_map/all_gather | solution.py:290
  369.7 97.1 %reduce-scatter.26.cloned.1.call-start = ((), (), s32[]{:S(2)}) async-start(), calls=%async_computation.28 | async-start | bytes 2949120 | tf_op jit(solution)/shard_map/reduce_scatter | solution.py:103
  433.6 68.8 %reduce-scatter.16.cloned.1.call-start = ((), (), s32[]{:S(2)}) async-start(), calls=%async_computation.20 | async-start | bytes 2949120 | tf_op jit(solution)/shard_map/reduce_scatter | solution.py:89
  439.3 98.8 %reduce-scatter.18.cloned.1.call-start = ((), (), s32[]{:S(2)}) async-start(), calls=%async_computation.22 | async-start | bytes 2949120 | tf_op jit(solution)/shard_map/reduce_scatter | solution.py:89
  445.7 196.4 %reduce-scatter.24.cloned.1.call-start = ((), (), s32[]{:S(2)}) async-start(), calls=%async_computation.26 | async-start | bytes 983040 | tf_op jit(solution)/shard_map/reduce_scatter | solution.py:344
  565.2 79.6 %reduce-scatter.30.cloned.1.call-start = ((), (), s32[]{:S(2)}) async-start(), calls=%async_computation.30 | async-start | bytes 983040 | tf_op jit(solution)/shard_map/reduce_scatter | solution.py:344
  590.2 58.1 %reduce-scatter.28.cloned.1.call-start = ((), (), s32[]{:S(2)}) async-start(), calls=%async_computation.29 | async-start | bytes 983040 | tf_op jit(solution)/shard_map/reduce_scatter | solution.py:338
  624.3 49.8 %reduce-scatter.22.cloned.1.call-start = ((), (), s32[]{:S(2)}) async-start(), calls=%async_computation.25 | async-start | bytes 983040 | tf_op jit(solution)/shard_map/reduce_scatter | solution.py:338
  642.0 101.4 %reduce-scatter.36.cloned.1.call-start = ((), (), s32[]{:S(2)}) async-start(), calls=%async_computation.33 | async-start | bytes 1990656 | tf_op jit(solution)/shard_map/reduce_scatter | solution.py:123
  648.3 164.0 %reduce-scatter.34.cloned.1.call-start = ((), (), s32[]{:S(2)}) async-start(), calls=%async_computation.32 | async-start | bytes 1990656 | tf_op jit(solution)/shard_map/reduce_scatter | solution.py:122
  678.9 240.1 %reduce-scatter.42.cloned.1.call-start = ((), (), s32[]{:S(2)}) async-start(), calls=%async_computation.36 | async-start | bytes 5971968 | tf_op jit(solution)/shard_map/reduce_scatter | solution.py:126
  684.6 342.2 %reduce-scatter.32.cloned.1.call-start = ((), (), s32[]{:S(2)}) async-start(), calls=%async_computation.31 | async-start | bytes 5971968 | tf_op jit(solution)/shard_map/reduce_scatter | solution.py:121
  704.5 415.5 %all-reduce.10.cloned.1.call-start = ((), (), s32[]{:S(2)}) async-start(), calls=%async_computation.38 | async-start | bytes 1769472 | tf_op jit(solution)/shard_map/psum | solution.py:430
  1028.7 120.4 %reduce-scatter.38.cloned.1.call-start = ((), (), s32[]{:S(2)}) async-start(), calls=%async_computation.34 | async-start | bytes 3981312 | tf_op jit(solution)/shard_map/reduce_scatter | solution.py:124
  1035.8 196.0 %reduce-scatter.40.cloned.1.call-start = ((), (), s32[]{:S(2)}) async-start(), calls=%async_computation.35 | async-start | bytes 3981312 | tf_op jit(solution)/shard_map/reduce_scatter | solution.py:125
  1044.3 270.2 %reduce-scatter.44.cloned.1.call-start = ((), (), s32[]{:S(2)}) async-start(), calls=%async_computation.37 | async-start | bytes 3981312 | tf_op jit(solution)/shard_map/reduce_scatter | solution.py:127
  (91 other events, 2012.1 us)
Sparse Core Ops, SparseCore 0:
  10.2 70.4 all-gather.8
  82.9 58.9 all-gather.10
  144.1 53.8 all-gather.16
  200.0 20.0 all-gather.12
  222.1 45.9 all-gather.14
  270.0 23.0 all-gather.20
  307.9 35.1 reduce-scatter.19
  369.0 24.1 all-gather.18
  394.8 24.0 all-gather.22
  433.7 33.0 reduce-scatter.25
  469.3 33.0 reduce-scatter.15
  505.0 33.0 reduce-scatter.17
  565.3 23.2 reduce-scatter.23
  591.1 23.2 reduce-scatter.29
  624.4 23.2 reduce-scatter.27
  650.9 23.2 reduce-scatter.21
  677.5 65.8 reduce-scatter.35
  747.1 65.0 reduce-scatter.33
  815.8 103.0 reduce-scatter.41
  922.8 103.9 reduce-scatter.31
  1030.0 35.1 all-reduce.9
  1069.4 79.6 reduce-scatter.37
  1153.3 78.4 reduce-scatter.39
  1235.8 78.6 reduce-scatter.43
